TPU v7x, 256 devices: a whole 4x4x8 slice. The times are simulated.
256 devices in a mesh: row: 64 (over z, x, core), col: 4 (over y).
Axes of the slice: x: 4, y: 4, z: 8, core: 2. Of those that a mesh axis runs over, the one named last changes fastest.
Arguments:
- right_sides: float32 [4, 256, 128, 128], P(None, 'row'), may hold values from -6 to 6
- inverse_diag: float32 [4, 256, 128, 128], P(None, 'row', 'col'), may hold values from -1 to 2
- lower_blocks: float32 [3, 256, 16, 128, 128], P(None, 'row', None, 'col'), may hold values from -0.09375 to 0.09375
- depends_on: int32 [3, 256, 16], replicated, may hold values from 0 to 255, as said below
Outputs:
- solution: float32 [4, 256, 128, 128], P(None, 'row', 'col')
Inputs may be any that keep to these rules, and one draw needn't show every extreme that they name: `depends_on`: in each level, the supernodes of one device along row name the supernodes of any one device along row at most 2 times in all, and some pair of devices reaches 2 in every level.
All inputs are finite; a program needn't handle non-finite values.
Results may differ from a plain program's by a relative error of at most 0.0001.
Values sent between devices are 32-bit elements; how exact they have to be, the bound alone decides.
A program may use at most 64 MiB of HBM per device.

v0:
```python
import jax
import jax.numpy as jnp
from jax import lax
from jax.sharding import PartitionSpec as P

exact_mode = lax.Precision.HIGHEST


def fetch_blocks(previous, wanted):
    shard_rows = lax.all_gather(previous, "row", axis=0, tiled=True)
    chooser = (wanted[:, None] == jnp.arange(shard_rows.shape[0], dtype=jnp.int32)[None, :]).astype(
        jnp.float32
    )
    return jnp.einsum("en,nrk->erk", chooser, shard_rows, precision=exact_mode)


def return_terms(terms, wanted, local_count):
    owners = (
        jnp.arange(local_count * lax.axis_size("row"), dtype=jnp.int32)[:, None] == wanted[None, :]
    ).astype(jnp.float32)
    return lax.psum_scatter(
        jnp.einsum("me,erk->mrk", owners, terms, precision=exact_mode),
        "row",
        scatter_dimension=0,
        tiled=True,
    )


def forward_update(partial_value):
    return lax.psum(partial_value, "col")


def backward_solve(inverse_level, rest):
    partial_value = jnp.einsum("jab,jak->jbk", inverse_level, rest, precision=exact_mode)
    return lax.psum(partial_value, "col")


def on_device(right_sides, inverse_diag, lower_blocks, depends_on):
    levels, local_count, width, columns = right_sides.shape
    share = inverse_diag.shape[2]
    fan_in = lower_blocks.shape[2]
    my_row = lax.axis_index("row")
    my_col = lax.axis_index("col")
    entries = local_count * fan_in
    wanted_all = [
        lax.dynamic_slice_in_dim(
            depends_on[level_no], my_row * local_count, local_count, 0
        ).reshape(entries)
        for level_no in range(levels - 1)
    ]
    solved_here = [
        jnp.einsum("jab,jbk->jak", inverse_diag[0], right_sides[0], precision=exact_mode)
    ]
    for level_no in range(1, levels):
        picked = fetch_blocks(solved_here[-1], wanted_all[level_no - 1])
        partial_value = jnp.einsum(
            "jdba,jdbk->jak",
            lower_blocks[level_no - 1],
            picked.reshape(local_count, fan_in, share, columns),
            precision=exact_mode,
        )
        update = forward_update(partial_value)
        residual = right_sides[level_no] - update
        solved_here.append(
            jnp.einsum("jab,jbk->jak", inverse_diag[level_no], residual, precision=exact_mode)
        )
    full_sol = backward_solve(inverse_diag[levels - 1], solved_here[levels - 1])
    pieces = [lax.dynamic_slice_in_dim(full_sol, my_col * share, share, 1)]
    for level_no in range(levels - 2, -1, -1):
        terms = jnp.einsum(
            "jdba,jak->jdbk", lower_blocks[level_no], full_sol, precision=exact_mode
        ).reshape(entries, share, columns)
        returned = return_terms(terms, wanted_all[level_no], local_count)
        rest = solved_here[level_no] - returned
        full_sol = backward_solve(inverse_diag[level_no], rest)
        pieces.insert(0, lax.dynamic_slice_in_dim(full_sol, my_col * share, share, 1))
    return jnp.stack(pieces)


def solution(mesh):
    return jax.shard_map(
        on_device,
        mesh=mesh,
        in_specs=(
            P(None, "row", None, None),
            P(None, "row", "col", None),
            P(None, "row", None, "col", None),
            P(),
        ),
        out_specs=P(None, "row", "col", None),
        check_vma=False,
    )
```

profile of v0, /device:TPU:2, one launch (start us, length us, event | category | flops | bytes accessed | tf_op | source)
XLA Modules:
  0.0 1079.7 jit_solution(4726448590712107465)
XLA Ops:
  9.6 3.6 fusion.65
  13.2 77.8 %all-gather.4.cloned.1.call-done = f32[256,32,128]{2,1,0:T(8,128)} async-done(((f32[4,32,128]{2,1,0:T(8,128)}), f32[256,32,128]{2,1,0:T(8,128)}) %all-gather.4.cloned.1.call-update) | async-done | bytes 4194320 | tf_op jit(solution)/shard_map/all_gather | solution.py:10
  91.0 6.2 fusion.4
  97.2 3.0 convolution_bitcast_fusion.6
  101.2 44.4 %all-reduce.8.cloned.1.call-done = f32[4,128,128]{1,2,0:T(8,128)} async-done(((f32[4,128,128]{1,2,0:T(8,128)}), f32[4,128,128]{1,2,0:T(8,128)}) %all-reduce.8.cloned.1.call-update) | async-done | bytes 262160 | tf_op jit(solution)/shard_map/psum | solution.py:30
  148.3 78.8 %all-gather.6.cloned.1.call-done = f32[256,32,128]{2,1,0:T(8,128)} async-done(((f32[4,32,128]{2,1,0:T(8,128)}), f32[256,32,128]{2,1,0:T(8,128)}) %all-gather.6.cloned.1.call-update) | async-done | bytes 4194320 | tf_op jit(solution)/shard_map/all_gather | solution.py:10
  227.1 6.1 fusion.2
  233.2 3.0 convolution_bitcast_fusion.5
  236.4 45.2 %all-reduce.10.cloned.1.call-done = f32[4,128,128]{1,2,0:T(8,128)} async-done(((f32[4,128,128]{1,2,0:T(8,128)}), f32[4,128,128]{1,2,0:T(8,128)}) %all-reduce.10.cloned.1.call-update) | async-done | bytes 262160 | tf_op jit(solution)/shard_map/psum | solution.py:30
  284.3 78.3 %all-gather.8.cloned.1.call-done = f32[256,32,128]{2,1,0:T(8,128)} async-done(((f32[4,32,128]{2,1,0:T(8,128)}), f32[256,32,128]{2,1,0:T(8,128)}) %all-gather.8.cloned.1.call-update) | async-done | bytes 4194320 | tf_op jit(solution)/shard_map/all_gather | solution.py:10
  362.6 6.1 fusion
  368.7 4.4 convolution_bitcast_fusion.4
  375.0 43.5 %all-reduce.12.cloned.1.call-done = f32[4,128,128]{1,2,0:T(8,128)} async-done(((f32[4,128,128]{1,2,0:T(8,128)}), f32[4,128,128]{1,2,0:T(8,128)}) %all-reduce.12.cloned.1.call-update) | async-done | bytes 262160 | tf_op jit(solution)/shard_map/psum | solution.py:30
  422.0 46.8 %all-reduce.14.cloned.1.call-done = f32[4,128,128]{1,2,0:T(8,128)} async-done(((f32[4,128,128]{1,2,0:T(8,128)}), f32[4,128,128]{1,2,0:T(8,128)}) %all-reduce.14.cloned.1.call-update) | async-done | bytes 262160 | tf_op jit(solution)/shard_map/psum | solution.py:35
  473.1 4.4 copy.45
  477.6 143.6 %reduce-scatter.4.cloned.1.call-done = f32[4,32,128]{2,1,0:T(8,128)} async-done(((f32[256,32,128]{2,1,0:T(8,128)}), f32[4,32,128]{2,1,0:T(8,128)}) %reduce-scatter.4.cloned.1.call-update) | async-done | bytes 65552 | tf_op jit(solution)/shard_map/reduce_scatter | solution.py:21
  623.5 46.0 %all-reduce.16.cloned.1.call-done = f32[4,128,128]{1,2,0:T(8,128)} async-done(((f32[4,128,128]{1,2,0:T(8,128)}), f32[4,128,128]{1,2,0:T(8,128)}) %all-reduce.16.cloned.1.call-update) | async-done | bytes 262160 | tf_op jit(solution)/shard_map/psum | solution.py:35
  671.5 2.3 fusion.14
  673.9 4.4 copy.49
  678.3 143.5 %reduce-scatter.6.cloned.1.call-done = f32[4,32,128]{2,1,0:T(8,128)} async-done(((f32[256,32,128]{2,1,0:T(8,128)}), f32[4,32,128]{2,1,0:T(8,128)}) %reduce-scatter.6.cloned.1.call-update) | async-done | bytes 65552 | tf_op jit(solution)/shard_map/reduce_scatter | solution.py:21
  824.3 46.0 %all-reduce.18.cloned.1.call-done = f32[4,128,128]{1,2,0:T(8,128)} async-done(((f32[4,128,128]{1,2,0:T(8,128)}), f32[4,128,128]{1,2,0:T(8,128)}) %all-reduce.18.cloned.1.call-update) | async-done | bytes 262160 | tf_op jit(solution)/shard_map/psum | solution.py:35
  874.6 4.4 copy.53
  879.1 143.5 %reduce-scatter.8.cloned.1.call-done = f32[4,32,128]{2,1,0:T(8,128)} async-done(((f32[256,32,128]{2,1,0:T(8,128)}), f32[4,32,128]{2,1,0:T(8,128)}) %reduce-scatter.8.cloned.1.call-update) | async-done | bytes 65552 | tf_op jit(solution)/shard_map/reduce_scatter | solution.py:21
  1025.5 45.5 %all-reduce.20.cloned.1.call-done = f32[4,128,128]{1,2,0:T(8,128)} async-done(((f32[4,128,128]{1,2,0:T(8,128)}), f32[4,128,128]{1,2,0:T(8,128)}) %all-reduce.20.cloned.1.call-update) | async-done | bytes 262160 | tf_op jit(solution)/shard_map/psum | solution.py:35
  (81 shorter events, 35.1 us)
Async XLA Ops:
  6.5 84.4 %all-gather.4.cloned.1.call-start = ((), (), s32[]{:S(2)}) async-start(), calls=%async_computation.3 | async-start | bytes 4259840 | tf_op jit(solution)/shard_map/all_gather | solution.py:10
  8.5 137.1 %all-reduce.8.cloned.1.call-start = ((), (), s32[]{:S(2)}) async-start(), calls=%async_computation.4 | async-start | bytes 524288 | tf_op jit(solution)/shard_map/psum | solution.py:30
  13.2 87.1 %copy-start.5 = (f32[4,4,128,128]{3,2,1,0:T(8,128)S(1)}, f32[4,4,128,128]{3,2,1,0:T(8,128)}, u32[]{:S(2)}) copy-start(f32[4,4,128,128]{3,2,1,0:T(8,128)} %param.4) | copy-start | bytes 3145732
  91.0 6.2 copy-start.6
  97.2 48.4 %copy-start.4 = (f32[4,4,32,128]{3,2,1,0:T(8,128)S(1)}, f32[4,4,32,128]{3,2,1,0:T(8,128)}, u32[]{:S(2)}) copy-start(f32[4,4,32,128]{3,2,1,0:T(8,128)} %param.5) | copy-start | bytes 786436
  100.2 126.9 %all-gather.6.cloned.1.call-start = ((), (), s32[]{:S(2)}) async-start(), calls=%async_computation.5 | async-start | bytes 4259840 | tf_op jit(solution)/shard_map/all_gather | solution.py:10
  147.7 133.9 %all-reduce.10.cloned.1.call-start = ((), (), s32[]{:S(2)}) async-start(), calls=%async_computation.6 | async-start | bytes 524288 | tf_op jit(solution)/shard_map/psum | solution.py:30
  236.3 126.3 %all-gather.8.cloned.1.call-start = ((), (), s32[]{:S(2)}) async-start(), calls=%async_computation.7 | async-start | bytes 4259840 | tf_op jit(solution)/shard_map/all_gather | solution.py:10
  283.7 134.8 %all-reduce.12.cloned.1.call-start = ((), (), s32[]{:S(2)}) async-start(), calls=%async_computation.8 | async-start | bytes 524288 | tf_op jit(solution)/shard_map/psum | solution.py:30
  368.7 100.1 %copy-start = (f32[3,4,16,32,128]{4,3,2,1,0:T(8,128)S(1)}, f32[3,4,16,32,128]{4,3,2,1,0:T(8,128)}, u32[]{:S(2)}) copy-start(f32[3,4,16,32,128]{4,3,2,1,0:T(8,128)} %param.6) | copy-start | bytes 9437188
  373.1 95.7 %all-reduce.14.cloned.1.call-start = ((), (), s32[]{:S(2)}) async-start(), calls=%async_computation.9 | async-start | bytes 524288 | tf_op jit(solution)/shard_map/psum | solution.py:35
  421.4 199.7 %reduce-scatter.4.cloned.1.call-start = ((), (), s32[]{:S(2)}) async-start(), calls=%async_computation.10 | async-start | bytes 4259840 | tf_op jit(solution)/shard_map/reduce_scatter | solution.py:21
  477.5 143.6 %copy-start.8 = (f32[4,32,128]{2,1,0:T(8,128)S(1)}, f32[4,32,128]{2,1,0:T(8,128)}, u32[]{:S(2)}) copy-start(f32[4,32,128]{2,1,0:T(8,128)} %convolution_bitcast_fusion.7) | copy-start | bytes 196612
  477.5 192.0 %all-reduce.16.cloned.1.call-start = ((), (), s32[]{:S(2)}) async-start(), calls=%async_computation.11 | async-start | bytes 524288 | tf_op jit(solution)/shard_map/psum | solution.py:35
  623.3 198.6 %reduce-scatter.6.cloned.1.call-start = ((), (), s32[]{:S(2)}) async-start(), calls=%async_computation.12 | async-start | bytes 4259840 | tf_op jit(solution)/shard_map/reduce_scatter | solution.py:21
  678.2 143.6 %copy-start.7 = (f32[4,32,128]{2,1,0:T(8,128)S(1)}, f32[4,32,128]{2,1,0:T(8,128)}, u32[]{:S(2)}) copy-start(f32[4,32,128]{2,1,0:T(8,128)} %convolution_bitcast_fusion.8) | copy-start | bytes 196612
  678.3 192.0 %all-reduce.18.cloned.1.call-start = ((), (), s32[]{:S(2)}) async-start(), calls=%async_computation.13 | async-start | bytes 524288 | tf_op jit(solution)/shard_map/psum | solution.py:35
  824.0 198.6 %reduce-scatter.8.cloned.1.call-start = ((), (), s32[]{:S(2)}) async-start(), calls=%async_computation.14 | async-start | bytes 4259840 | tf_op jit(solution)/shard_map/reduce_scatter | solution.py:21
  879.0 143.6 %copy-start.9 = (f32[4,32,128]{2,1,0:T(8,128)S(1)}, f32[4,32,128]{2,1,0:T(8,128)}, u32[]{:S(2)}) copy-start(f32[4,32,128]{2,1,0:T(8,128)} %fusion.22) | copy-start | bytes 196612
  879.0 145.8 %copy-start.1 = (f32[4,128,128]{1,2,0:T(8,128)S(1)}, f32[4,128,128]{1,2,0:T(8,128)}, u32[]{:S(2)}) copy-start(f32[4,128,128]{1,2,0:T(8,128)} %all-reduce.14.cloned.1.call-done) | copy-start | bytes 786436
  879.0 146.0 %copy-start.2 = (f32[4,128,128]{1,2,0:T(8,128)S(1)}, f32[4,128,128]{1,2,0:T(8,128)}, u32[]{:S(2)}) copy-start(f32[4,128,128]{1,2,0:T(8,128)} %all-reduce.16.cloned.1.call-done) | copy-start | bytes 786436
  879.0 146.3 %copy-start.3 = (f32[4,128,128]{1,2,0:T(8,128)S(1)}, f32[4,128,128]{1,2,0:T(8,128)}, u32[]{:S(2)}) copy-start(f32[4,128,128]{1,2,0:T(8,128)} %all-reduce.18.cloned.1.call-done) | copy-start | bytes 786436
  879.0 192.0 %all-reduce.20.cloned.1.call-start = ((), (), s32[]{:S(2)}) async-start(), calls=%async_computation.15 | async-start | bytes 524288 | tf_op jit(solution)/shard_map/psum | solution.py:35
Sparse Core Ops, SparseCore 0:
  10.1 80.7 all-gather.3
  100.3 45.2 all-reduce.7
  148.7 78.3 all-gather.5
  236.4 45.1 all-reduce.9
  284.2 78.3 all-gather.7
  373.2 45.2 all-reduce.11
  421.5 47.2 all-reduce.13
  477.6 143.4 reduce-scatter.3
  623.6 45.9 all-reduce.15
  678.4 143.4 reduce-scatter.5
  824.3 45.9 all-reduce.17
  879.1 143.4 reduce-scatter.7
  1025.0 45.9 all-reduce.19
where the time goes:
time: 1090 us; the launch traced here: 1080 us
  waiting for transfers between devices  983 us (90%)
  matrix products  57.1 us (5%)
  local copies, waits for them, and re-layouts  22.8 us (2%)
  between operations  13.7 us (1%)
    reduce_scatter x3, waiting for transfers between devices, return_terms(): lax.psum_scatter(jnp.einsum('me,erk->mrk', owners, terms, precision=exact...  431 us
    all_gather x3, waiting for transfers between devices, fetch_blocks(): shard_rows = lax.all_gather(previous, 'row', axis=0, tiled=True)  235 us
    psum x4, waiting for transfers between devices, backward_solve(): return lax.psum(partial_value, 'col')  184 us
    psum x3, waiting for transfers between devices, forward_update(): return lax.psum(partial_value, 'col')  133 us
  transfers between devices with their start and end apart: 13, of which 13 were waited for; matrix products, arithmetic and copies ran while one was open for 1% of the time, Pallas kernels for 0%

commit v1 on v0

--- a/solution.py
+++ b/solution.py
@@ -7,7 +7,8 @@
 
 
 def fetch_blocks(previous, wanted):
-    shard_rows = lax.all_gather(previous, "row", axis=0, tiled=True)
+    sent = jnp.stack([previous] * lax.axis_size("row"))
+    shard_rows = jnp.concatenate(lax.all_to_all(sent, "row", 0, 0), axis=0)
     chooser = (wanted[:, None] == jnp.arange(shard_rows.shape[0], dtype=jnp.int32)[None, :]).astype(
         jnp.float32
     )

time: 1090 us -> 1170 us (1.073)
  waiting for transfers between devices: 983 us -> 1030 us
  starting transfers between devices: 2.1 us -> 35.8 us
    all_to_all x0 -> x3, waiting for transfers between devices: none -> 285 us  [fetch_blocks(): shard_rows = jnp.concatenate(lax.all_to_all(sent, 'row', 0, 0), axis=0)]
    all_gather x3 -> x0, waiting for transfers between devices: 235 us -> none  [fetch_blocks(): shard_rows = lax.all_gather(previous, 'row', axis=0, tiled=True)]
    all_to_all x0 -> x3, starting transfers between devices: none -> 33.9 us  [fetch_blocks(): shard_rows = jnp.concatenate(lax.all_to_all(sent, 'row', 0, 0), axis=0)]
  transfers between devices with their start and end apart: 13 -> 13, of which waited for: 13 -> 13; matrix products, arithmetic and copies ran while one was open for 1% -> 0% of each run, Pallas kernels for 0% -> 0%
where the time goes in v1:
time: 1170 us; the launch traced here: 1160 us
  waiting for transfers between devices  1030 us (88%)
  matrix products  53.5 us (5%)
  starting transfers between devices  35.8 us (3%)
  local copies, waits for them, and re-layouts  26.2 us (2%)
  between operations  14.2 us (1%)
    reduce_scatter x3, waiting for transfers between devices, return_terms(): lax.psum_scatter(jnp.einsum('me,erk->mrk', owners, terms, precision=exact...  431 us
    all_to_all x3, waiting for transfers between devices, fetch_blocks(): shard_rows = jnp.concatenate(lax.all_to_all(sent, 'row', 0, 0), axis=0)  285 us
    psum x4, waiting for transfers between devices, backward_solve(): return lax.psum(partial_value, 'col')  184 us
    psum x3, waiting for transfers between devices, forward_update(): return lax.psum(partial_value, 'col')  128 us
    all_to_all x3, starting transfers between devices, fetch_blocks(): shard_rows = jnp.concatenate(lax.all_to_all(sent, 'row', 0, 0), axis=0)  33.9 us
  transfers between devices with their start and end apart: 13, of which 13 were waited for; matrix products, arithmetic and copies ran while one was open for 0% of the time, Pallas kernels for 0%

profile of v1, /device:TPU:2, one launch (start us, length us, event | category | flops | bytes accessed | tf_op | source)
XLA Modules:
  0.0 1158.2 jit_solution(10139087442771048965)
XLA Ops:
  11.0 12.5 %all-to-all-start = ((f32[64,4,32,128]{3,2,1,0:T(8,128)}), f32[64,4,32,128]{3,2,1,0:T(8,128)}, u32[]{:S(2)}, u32[]{:S(2)}) async-start(f32[64,4,32,128]{3,2,1,0:T(8,128)} %stack.16), calls=%async_computation | async-start | bytes 8388608 | tf_op jit(solution)/shard_map/all_to_all | solution.py:11
  25.5 94.1 %all-to-all-done = f32[64,4,32,128]{3,2,1,0:T(8,128)} async-done(((f32[64,4,32,128]{3,2,1,0:T(8,128)}), f32[64,4,32,128]{3,2,1,0:T(8,128)}, u32[]{:S(2)}, u32[]{:S(2)}) %all-to-all-start) | async-done | bytes 4194336 | tf_op jit(solution)/shard_map/all_to_all | solution.py:11
  119.6 6.2 fusion.4
  128.8 43.3 %all-reduce.8.cloned.1.call-done = f32[4,128,128]{2,1,0:T(8,128)} async-done(((f32[4,128,128]{2,1,0:T(8,128)}), f32[4,128,128]{2,1,0:T(8,128)}) %all-reduce.8.cloned.1.call-update) | async-done | bytes 262160 | tf_op jit(solution)/shard_map/psum | solution.py:31
  176.1 10.7 all-to-all-start.1
  187.6 95.4 %all-to-all-done.1 = f32[64,4,32,128]{3,2,1,0:T(8,128)} async-done(((f32[64,4,32,128]{3,2,1,0:T(8,128)}), f32[64,4,32,128]{3,2,1,0:T(8,128)}, u32[]{:S(2)}, u32[]{:S(2)}) %all-to-all-start.1) | async-done | bytes 4194336 | tf_op jit(solution)/shard_map/all_to_all | solution.py:11
  282.9 6.2 fusion.2
  289.1 3.0 convolution_bitcast_fusion.5
  292.2 42.4 %all-reduce.10.cloned.1.call-done = f32[4,128,128]{2,1,0:T(8,128)} async-done(((f32[4,128,128]{2,1,0:T(8,128)}), f32[4,128,128]{2,1,0:T(8,128)}) %all-reduce.10.cloned.1.call-update) | async-done | bytes 262160 | tf_op jit(solution)/shard_map/psum | solution.py:31
  338.4 10.7 all-to-all-start.2
  350.0 95.3 %all-to-all-done.2 = f32[64,4,32,128]{3,2,1,0:T(8,128)} async-done(((f32[64,4,32,128]{3,2,1,0:T(8,128)}), f32[64,4,32,128]{3,2,1,0:T(8,128)}, u32[]{:S(2)}, u32[]{:S(2)}) %all-to-all-start.2) | async-done | bytes 4194336 | tf_op jit(solution)/shard_map/all_to_all | solution.py:11
  445.3 6.2 fusion
  451.5 3.0 convolution_bitcast_fusion.4
  454.6 42.3 %all-reduce.12.cloned.1.call-done = f32[4,128,128]{2,1,0:T(8,128)} async-done(((f32[4,128,128]{2,1,0:T(8,128)}), f32[4,128,128]{2,1,0:T(8,128)}) %all-reduce.12.cloned.1.call-update) | async-done | bytes 262160 | tf_op jit(solution)/shard_map/psum | solution.py:31
  500.0 47.1 %all-reduce.14.cloned.1.call-done = f32[4,128,128]{1,2,0:T(8,128)} async-done(((f32[4,128,128]{1,2,0:T(8,128)}), f32[4,128,128]{1,2,0:T(8,128)}) %all-reduce.14.cloned.1.call-update) | async-done | bytes 262160 | tf_op jit(solution)/shard_map/psum | solution.py:36
  551.3 4.4 copy.47
  555.7 143.5 %reduce-scatter.4.cloned.1.call-done = f32[4,32,128]{2,1,0:T(8,128)} async-done(((f32[256,32,128]{2,1,0:T(8,128)}), f32[4,32,128]{2,1,0:T(8,128)}) %reduce-scatter.4.cloned.1.call-update) | async-done | bytes 65552 | tf_op jit(solution)/shard_map/reduce_scatter | solution.py:22
  701.8 45.8 %all-reduce.16.cloned.1.call-done = f32[4,128,128]{1,2,0:T(8,128)} async-done(((f32[4,128,128]{1,2,0:T(8,128)}), f32[4,128,128]{1,2,0:T(8,128)}) %all-reduce.16.cloned.1.call-update) | async-done | bytes 262160 | tf_op jit(solution)/shard_map/psum | solution.py:36
  751.8 4.4 copy.50
  756.3 143.5 %reduce-scatter.6.cloned.1.call-done = f32[4,32,128]{2,1,0:T(8,128)} async-done(((f32[256,32,128]{2,1,0:T(8,128)}), f32[4,32,128]{2,1,0:T(8,128)}) %reduce-scatter.6.cloned.1.call-update) | async-done | bytes 65552 | tf_op jit(solution)/shard_map/reduce_scatter | solution.py:22
  902.4 45.9 %all-reduce.18.cloned.1.call-done = f32[4,128,128]{1,2,0:T(8,128)} async-done(((f32[4,128,128]{1,2,0:T(8,128)}), f32[4,128,128]{1,2,0:T(8,128)}) %all-reduce.18.cloned.1.call-update) | async-done | bytes 262160 | tf_op jit(solution)/shard_map/psum | solution.py:36
  952.6 4.4 copy.53
  957.0 143.5 %reduce-scatter.8.cloned.1.call-done = f32[4,32,128]{2,1,0:T(8,128)} async-done(((f32[256,32,128]{2,1,0:T(8,128)}), f32[4,32,128]{2,1,0:T(8,128)}) %reduce-scatter.8.cloned.1.call-update) | async-done | bytes 65552 | tf_op jit(solution)/shard_map/reduce_scatter | solution.py:22
  1103.4 45.5 %all-reduce.20.cloned.1.call-done = f32[4,128,128]{1,2,0:T(8,128)} async-done(((f32[4,128,128]{1,2,0:T(8,128)}), f32[4,128,128]{1,2,0:T(8,128)}) %all-reduce.20.cloned.1.call-update) | async-done | bytes 262160 | tf_op jit(solution)/shard_map/psum | solution.py:36
  (81 shorter events, 44.8 us)
Async XLA Ops:
  11.0 12.5 %copy-start.10 = (s32[3,256,16]{1,2,0:T(8,128)S(1)}, s32[3,256,16]{1,2,0:T(8,128)}, u32[]{:S(2)}) copy-start(s32[3,256,16]{1,2,0:T(8,128)} %param.7) | copy-start | bytes 147460
  11.0 12.7 %copy-start = (f32[3,4,16,32,128]{4,3,2,1,0:T(8,128)S(1)}, f32[3,4,16,32,128]{4,3,2,1,0:T(8,128)}, u32[]{:S(2)}) copy-start(f32[3,4,16,32,128]{4,3,2,1,0:T(8,128)} %param.6) | copy-start | bytes 9437188
  11.0 108.6 %all-to-all-start = ((f32[64,4,32,128]{3,2,1,0:T(8,128)}), f32[64,4,32,128]{3,2,1,0:T(8,128)}, u32[]{:S(2)}, u32[]{:S(2)}) async-start(f32[64,4,32,128]{3,2,1,0:T(8,128)} %stack.16), calls=%async_computation | async-start | bytes 8388608 | tf_op jit(solution)/shard_map/all_to_all | solution.py:11
  23.5 148.7 %all-reduce.8.cloned.1.call-start = ((), (), s32[]{:S(2)}) async-start(), calls=%async_computation.6 | async-start | bytes 524288 | tf_op jit(solution)/shard_map/psum | solution.py:31
  25.5 146.7 %copy-start.7 = (f32[4,4,32,128]{3,2,1,0:T(8,128)S(1)}, f32[4,4,32,128]{3,2,1,0:T(8,128)}, u32[]{:S(2)}) copy-start(f32[4,4,32,128]{3,2,1,0:T(8,128)} %param.5) | copy-start | bytes 786436
  119.6 6.2 copy-start.3
  176.1 106.9 %all-to-all-start.1 = ((f32[64,4,32,128]{3,2,1,0:T(8,128)}), f32[64,4,32,128]{3,2,1,0:T(8,128)}, u32[]{:S(2)}, u32[]{:S(2)}) async-start(f32[64,4,32,128]{3,2,1,0:T(8,128)} %stack.17), calls=%async_computation.1 | async-start | bytes 8388608 | tf_op jit(solution)/shard_map/all_to_all | solution.py:11
  186.8 147.7 %all-reduce.10.cloned.1.call-start = ((), (), s32[]{:S(2)}) async-start(), calls=%async_computation.7 | async-start | bytes 524288 | tf_op jit(solution)/shard_map/psum | solution.py:31
  282.9 6.2 copy-start.2
  338.4 106.9 %all-to-all-start.2 = ((f32[64,4,32,128]{3,2,1,0:T(8,128)}), f32[64,4,32,128]{3,2,1,0:T(8,128)}, u32[]{:S(2)}, u32[]{:S(2)}) async-start(f32[64,4,32,128]{3,2,1,0:T(8,128)} %stack.18), calls=%async_computation.2 | async-start | bytes 8388608 | tf_op jit(solution)/shard_map/all_to_all | solution.py:11
  349.2 147.7 %all-reduce.12.cloned.1.call-start = ((), (), s32[]{:S(2)}) async-start(), calls=%async_computation.8 | async-start | bytes 524288 | tf_op jit(solution)/shard_map/psum | solution.py:31
  445.3 6.2 copy-start.1
  445.3 54.6 %copy-start.11 = (s32[1,4,16]{2,1,0:T(4,128)S(1)}, s32[1,4,16]{2,1,0:T(4,128)}, u32[]{:S(2)}) copy-start(s32[1,4,16]{2,1,0:T(4,128)} %copy.18) | copy-start | bytes 772
  454.6 92.5 %all-reduce.14.cloned.1.call-start = ((), (), s32[]{:S(2)}) async-start(), calls=%async_computation.9 | async-start | bytes 524288 | tf_op jit(solution)/shard_map/psum | solution.py:36
  499.6 199.6 %reduce-scatter.4.cloned.1.call-start = ((), (), s32[]{:S(2)}) async-start(), calls=%async_computation.10 | async-start | bytes 4259840 | tf_op jit(solution)/shard_map/reduce_scatter | solution.py:22
  555.7 191.9 %all-reduce.16.cloned.1.call-start = ((), (), s32[]{:S(2)}) async-start(), calls=%async_computation.11 | async-start | bytes 524288 | tf_op jit(solution)/shard_map/psum | solution.py:36
  701.4 198.4 %reduce-scatter.6.cloned.1.call-start = ((), (), s32[]{:S(2)}) async-start(), calls=%async_computation.12 | async-start | bytes 4259840 | tf_op jit(solution)/shard_map/reduce_scatter | solution.py:22
  756.2 192.1 %all-reduce.18.cloned.1.call-start = ((), (), s32[]{:S(2)}) async-start(), calls=%async_computation.13 | async-start | bytes 524288 | tf_op jit(solution)/shard_map/psum | solution.py:36
  902.0 198.5 %reduce-scatter.8.cloned.1.call-start = ((), (), s32[]{:S(2)}) async-start(), calls=%async_computation.14 | async-start | bytes 4259840 | tf_op jit(solution)/shard_map/reduce_scatter | solution.py:22
  956.9 143.6 %copy-start.9 = (f32[4,32,128]{2,1,0:T(8,128)S(1)}, f32[4,32,128]{2,1,0:T(8,128)}, u32[]{:S(2)}) copy-start(f32[4,32,128]{2,1,0:T(8,128)} %copy-done.8) | copy-start | bytes 196612
  956.9 145.8 %copy-start.4 = (f32[4,128,128]{1,2,0:T(8,128)S(1)}, f32[4,128,128]{1,2,0:T(8,128)}, u32[]{:S(2)}) copy-start(f32[4,128,128]{1,2,0:T(8,128)} %all-reduce.14.cloned.1.call-done) | copy-start | bytes 786436
  956.9 146.0 %copy-start.5 = (f32[4,128,128]{1,2,0:T(8,128)S(1)}, f32[4,128,128]{1,2,0:T(8,128)}, u32[]{:S(2)}) copy-start(f32[4,128,128]{1,2,0:T(8,128)} %all-reduce.16.cloned.1.call-done) | copy-start | bytes 786436
  956.9 146.3 %copy-start.6 = (f32[4,128,128]{1,2,0:T(8,128)S(1)}, f32[4,128,128]{1,2,0:T(8,128)}, u32[]{:S(2)}) copy-start(f32[4,128,128]{1,2,0:T(8,128)} %all-reduce.18.cloned.1.call-done) | copy-start | bytes 786436
  957.0 191.9 %all-reduce.20.cloned.1.call-start = ((), (), s32[]{:S(2)}) async-start(), calls=%async_computation.15 | async-start | bytes 524288 | tf_op jit(solution)/shard_map/psum | solution.py:36
  (1 other events, 0.6 us)
Sparse Core Ops, SparseCore 0:
  129.0 43.1 all-reduce.7
  292.3 42.1 all-reduce.9
  454.7 42.1 all-reduce.11
  499.7 47.2 all-reduce.13
  555.8 143.3 reduce-scatter.3
  701.5 46.0 all-reduce.15
  756.3 143.4 reduce-scatter.5
  902.2 46.0 all-reduce.17
  957.1 143.3 reduce-scatter.7
  1102.8 46.0 all-reduce.19
